TPU v7x, 128 devices: a whole 4x4x4 slice. The times are simulated.
128 devices in a mesh: ctx: 16 (over x, y_hi, core), tp: 8 (over y_lo, z).
Axes of the slice: x: 4, y: 4 (y_hi: 2, y_lo: 2; y = y_hi * 2 + y_lo), z: 4, core: 2. Of those that a mesh axis runs over, the one named last changes fastest.
Arguments:
- queries: bfloat16 [4096, 8192], P('ctx', 'tp'), may hold values from -120 to 120
- key_proj: bfloat16 [4096, 1024], P('ctx', 'tp'), may hold values from -4 to 4
- value_proj: bfloat16 [4096, 1024], P('ctx', 'tp'), may hold values from -6 to 6
- out_weight: bfloat16 [8192, 8192], P('tp'), may hold values from -0.75 to 0.75
- doc_ids: int32 [4096], replicated, may hold values from 0 to 7, never falling along the last dimension, each value on 1 to 2048 neighbouring positions
- drop_seed: int32 [1], replicated, may hold values from 0 to 1073741823
Outputs:
- output: bfloat16 [4096, 8192], P('ctx', 'tp')
Inputs may be any that keep to these rules, and one draw needn't show every extreme that they name: doc_ids never fall along the sequence; each document has 1 to 2048 tokens, one exactly 2048.
All inputs are finite; a program needn't handle non-finite values.
Results may differ from a plain program's by a relative error of at most 0.019.
Values may be sent and summed in bfloat16 or wider, within the bound.
No kernel may reach another device: no remote copies, remote signals or barrier semaphores. Data moves between devices by JAX's collectives and lax.ppermute only.
A program may use at most 128 MiB of HBM per device.

v0:
```python
import math
import jax
import jax.numpy as jnp
from jax import lax
from jax.sharding import PartitionSpec as P

HEADS = 64
KVH = 8
HD = 128


def mixing(value):
    value = value ^ lax.shift_right_logical(value, jnp.int32(16))
    value = value * 73244475
    value = value ^ lax.shift_right_logical(value, jnp.int32(16))
    value = value * 73244475
    value = value ^ lax.shift_right_logical(value, jnp.int32(16))
    return value


def attend_tile(state, context, k_block, v_block, k_start):
    q_heads, q_pos, q_doc, q_hash, doc_ids = context
    count = k_block.shape[0]
    local_kv = q_heads.shape[1]
    k_pos = k_start + jnp.arange(count, dtype=jnp.int32)
    k_doc = lax.dynamic_slice_in_dim(doc_ids, k_start, count)
    peak, row_sum, accum = state
    k_heads = k_block.reshape(count, local_kv, HD)
    v_heads = v_block.reshape(count, local_kv, HD)
    scores = jnp.einsum(
        "qkgd,nkd->qkgn", q_heads, k_heads, preferred_element_type=jnp.float32
    ) * HD ** (-0.5)
    allowed = (q_doc[:, None] == k_doc[None, :]) & (k_pos[None, :] <= q_pos[:, None])
    allowed = allowed[:, None, None, :]
    row_max = jnp.max(jnp.where(allowed, scores, jnp.float32(-1e30)), axis=-1)
    new_peak = jnp.maximum(peak, row_max)
    rescale = jnp.exp(peak - new_peak)
    weights = jnp.where(allowed, jnp.exp(scores - new_peak[..., None]), jnp.float32(0.0))
    row_sum = row_sum * rescale + jnp.sum(weights, axis=-1)
    full_hash = mixing(q_hash + k_pos.reshape(1, 1, 1, count))
    keeper = lax.shift_right_logical(full_hash, jnp.int32(8)) >= 1677722
    dropped = jnp.where(keeper, weights * jnp.float32(1.0 / 0.9), jnp.float32(0.0)).astype(
        jnp.bfloat16
    )
    accum = accum * rescale[..., None] + jnp.einsum(
        "qkgn,nkd->qkgd", dropped, v_heads, preferred_element_type=jnp.float32
    )
    return (new_peak, row_sum, accum)


def attend_range(state, context, k_rows, v_rows):
    count = k_rows.shape[0]
    tile_rows = math.gcd(count, 512)

    def step_tile(number, current):
        offset = number * tile_rows
        k_tile = lax.dynamic_slice_in_dim(k_rows, offset, tile_rows, 0)
        v_tile = lax.dynamic_slice_in_dim(v_rows, offset, tile_rows, 0)
        return attend_tile(current, context, k_tile, v_tile, offset)

    return lax.fori_loop(0, count // tile_rows, step_tile, state)


def body(queries, key_proj, value_proj, out_weight, doc_ids, drop_seed):
    tok_rows = queries.shape[0]
    half_rows = tok_rows // 2
    local_kv = key_proj.shape[1] // HD
    per_group = HEADS // KVH
    ctx_index = lax.axis_index("ctx")
    tp_index = lax.axis_index("tp")
    head_ids = tp_index * (local_kv * per_group) + jnp.arange(local_kv * per_group, dtype=jnp.int32)
    head_ids = head_ids.reshape(1, local_kv, per_group, 1)
    seed_value = drop_seed[0]
    half_index = jnp.arange(half_rows, dtype=jnp.int32)
    first_q = queries[:half_rows]
    second_q = queries[half_rows:]
    first_pos = ctx_index * tok_rows + half_index
    second_pos = ctx_index * tok_rows + half_rows + half_index
    contexts = []
    for half_q, half_pos in ((first_q, first_pos), (second_q, second_pos)):
        q_heads = half_q.reshape(half_rows, local_kv, per_group, HD)
        q_doc = lax.dynamic_slice_in_dim(doc_ids, half_pos[0], half_rows)
        q_hash = mixing(
            mixing(seed_value * 7919 + head_ids) ^ half_pos.reshape(half_rows, 1, 1, 1) * 65537
        )
        contexts.append((q_heads, half_pos, q_doc, q_hash, doc_ids))

    def start_state():
        return (
            jnp.full((half_rows, local_kv, per_group), -1e30, jnp.float32),
            jnp.zeros((half_rows, local_kv, per_group), jnp.float32),
            jnp.zeros((half_rows, local_kv, per_group, HD), jnp.float32),
        )

    piece = (
        lax.all_gather(key_proj, "ctx", axis=0, tiled=True),
        lax.all_gather(value_proj, "ctx", axis=0, tiled=True),
    )
    final = (
        attend_range(start_state(), contexts[0], piece[0], piece[1]),
        attend_range(start_state(), contexts[1], piece[0], piece[1]),
    )
    halves = []
    for state in final:
        peak, row_sum, accum = state
        halves.append(
            (accum / row_sum[..., None])
            .astype(jnp.bfloat16)
            .reshape(half_rows, local_kv * per_group * HD)
        )
    second_rows = halves[1]
    attention = jnp.concatenate([halves[0], second_rows], axis=0)
    partial_value = jnp.dot(attention, out_weight, preferred_element_type=jnp.float32)
    return lax.psum_scatter(
        partial_value.astype(jnp.bfloat16), "tp", scatter_dimension=1, tiled=True
    )


def solution(mesh):
    in_specs = (P("ctx", "tp"), P("ctx", "tp"), P("ctx", "tp"), P("tp", None), P(), P())
    out_specs = P("ctx", "tp")
    return jax.shard_map(body, mesh=mesh, in_specs=in_specs, out_specs=out_specs, check_vma=False)
```

profile of v0, /device:TPU:1, one launch (start us, length us, event | category | flops | bytes accessed | tf_op | source)
XLA Modules:
  0.0 272.1 jit_solution(3087980518251727780)
XLA Ops:
  7.3 1.6 copy.13
  9.2 1.1 fusion.74
  11.8 0.9 fusion.75
  12.6 45.7 %all-gather.3.cloned.1.call-done = bf16[4096,128]{1,0:T(8,128)(2,1)} async-done(((bf16[256,128]{1,0:T(8,128)(2,1)}), bf16[4096,128]{1,0:T(8,128)(2,1)}) %all-gather.3.cloned.1.call-update) | async-done | bytes 1048592 | tf_op jit(solution)/shard_map/all_gather | solution.py:96
  58.4 46.4 %all-gather.5.cloned.1.call-done = bf16[4096,128]{0,1:T(8,128)(2,1)} async-done(((bf16[256,128]{0,1:T(8,128)(2,1)}), bf16[4096,128]{0,1:T(8,128)(2,1)}) %all-gather.5.cloned.1.call-update) | async-done | bytes 1048592 | tf_op jit(solution)/shard_map/all_gather | solution.py:97
  104.7 53.2 %while.37 = (s32[]{:T(128)}, f32[128,1,8]{0,2,1:T(8,128)S(1)}, f32[128,1,8]{0,2,1:T(8,128)S(1)}, f32[128,1,8,128]{0,3,2,1:T(8,128)}, s32[128]{0:T(128)S(1)}, /*i...) while((s32[]{:T(128)}, f32[128,1,8]{0,2,1:T(8,128)S(1)}, ...), condition=%wide.region_7.8_spmd.clone, body=%wide.region_4.7_spmd.clone.sunk | while | flops 281624192 | bytes 12409155 | solution.py:61
  104.8 0.8 dynamic_slice.89
  105.7 1.4 fusion.100
  108.1 2.4 fusion.104
  110.6 0.8 copy-done.1
  111.4 0.8 dynamic_slice.89
  112.4 1.4 fusion.100
  114.8 2.4 fusion.104
  117.3 0.8 copy-done.1
  118.1 0.8 dynamic_slice.89
  119.0 1.4 fusion.100
  121.4 2.4 fusion.104
  123.9 0.8 copy-done.1
  124.7 0.8 dynamic_slice.89
  125.7 1.4 fusion.100
  128.1 2.4 fusion.104
  130.6 0.8 copy-done.1
  131.3 0.8 dynamic_slice.89
  132.3 1.4 fusion.100
  134.7 2.4 fusion.104
  137.2 0.8 copy-done.1
  138.0 0.8 dynamic_slice.89
  139.0 1.4 fusion.100
  141.4 2.4 fusion.104
  143.9 0.8 copy-done.1
  144.6 0.8 dynamic_slice.89
  145.6 1.4 fusion.100
  148.0 2.4 fusion.104
  150.5 0.8 copy-done.1
  152.3 1.4 fusion.100
  154.7 2.4 fusion.104
  157.2 0.8 copy-done.1
  157.9 43.4 %while.36 = (s32[]{:T(128)}, f32[128,1,8]{0,2,1:T(8,128)S(1)}, f32[128,1,8]{0,2,1:T(8,128)S(1)}, f32[128,1,8,128]{0,3,2,1:T(8,128)S(1)}, s32[128]{0:T(128)S(1)},...) while((s32[]{:T(128)}, f32[128,1,8]{0,2,1:T(8,128)S(1)}, ...), condition=%wide.region_3.4_spmd.clone, body=%wide.region_0.3_spmd.clone.sunk | while | flops 281624192 | bytes 8214795 | solution.py:61
  158.0 0.8 dynamic_slice.86
  159.0 1.4 fusion.93
  160.9 2.4 fusion.97
  163.4 0.8 dynamic_slice.86
  164.4 1.4 fusion.93
  166.4 2.4 fusion.97
  168.9 0.8 dynamic_slice.86
  169.8 1.4 fusion.93
  171.8 2.4 fusion.97
  174.3 0.8 dynamic_slice.86
  175.2 1.4 fusion.93
  177.2 2.4 fusion.97
  179.7 0.8 dynamic_slice.86
  180.7 1.4 fusion.93
  182.6 2.4 fusion.97
  185.1 0.8 dynamic_slice.86
  186.1 1.4 fusion.93
  188.0 2.4 fusion.97
  190.5 0.8 dynamic_slice.86
  191.5 1.4 fusion.93
  193.5 2.4 fusion.97
  196.0 0.8 dynamic_slice.86
  196.9 1.4 fusion.93
  198.9 2.4 fusion.97
  201.5 12.1 %convolution_convert_fusion = bf16[256,8192]{1,0:T(8,128)(2,1)} fusion(bf16[1024,8192]{1,0:T(8,128)(2,1)} %param.13, bf16[128,1024]{0,1:T(8,128)(2,1)S(1)} %bitcast.164, bf16[128,1024]{0,1:T(8,128)(2,1)S(1)} %bitcast.165), kind=kOutput, calls=%fused_computation.100 | convolution fusion | flops 4298113024 | bytes 21495808 | tf_op jit(solution)/shard_map/dot_general | solution.py:113
  213.6 51.9 %reduce-scatter.2.cloned.1.call-done = bf16[256,1024]{1,0:T(8,128)(2,1)} async-done(((bf16[256,8192]{1,0:T(8,128)(2,1)}), bf16[256,1024]{1,0:T(8,128)(2,1)}) %reduce-scatter.2.cloned.1.call-update) | async-done | bytes 524304 | tf_op jit(solution)/shard_map/reduce_scatter | solution.py:114
  (177 shorter events, 18.3 us)
Async XLA Ops:
  6.5 51.8 %all-gather.3.cloned.1.call-start = ((), (), s32[]{:S(2)}) async-start(), calls=%async_computation.1 | async-start | bytes 1114112 | tf_op jit(solution)/shard_map/all_gather | solution.py:96
  7.3 97.5 %all-gather.5.cloned.1.call-start = ((), (), s32[]{:S(2)}) async-start(), calls=%async_computation.2 | async-start | bytes 1114112 | tf_op jit(solution)/shard_map/all_gather | solution.py:97
  8.9 256.6 %reduce-scatter.2.cloned.1.call-start = ((), (), s32[]{:S(2)}) async-start(), calls=%async_computation.3 | async-start | bytes 4718592 | tf_op jit(solution)/shard_map/reduce_scatter | solution.py:114
  107.1 1.0 copy-start
  110.6 0.8 copy-start.1
  113.8 1.0 copy-start
  117.2 0.8 copy-start.1
  120.4 1.0 copy-start
  123.9 0.8 copy-start.1
  127.0 1.0 copy-start
  130.5 0.8 copy-start.1
  133.7 1.0 copy-start
  137.2 0.8 copy-start.1
  140.3 1.0 copy-start
  143.8 0.8 copy-start.1
  147.0 1.0 copy-start
  150.5 0.8 copy-start.1
  153.6 1.0 copy-start
  157.1 0.8 copy-start.1
  157.9 43.4 %copy-start.2 = (f32[128,1,8,128]{0,3,2,1:T(8,128)S(1)}, f32[128,1,8,128]{0,3,2,1:T(8,128)}, u32[]{:S(2)}) copy-start(f32[128,1,8,128]{0,3,2,1:T(8,128)} %get-tuple-element.377) | copy-start | bytes 1572868
Sparse Core Ops, SparseCore 0:
  9.8 48.5 all-gather.2
  60.6 44.0 all-gather.4
  213.7 51.7 reduce-scatter.1
where the time goes:
time: 274 us; the launch traced here: 272 us
  waiting for transfers between devices  145 us (53%)
  matrix products  73.1 us (27%)
  local copies, waits for them, and re-layouts  25.6 us (9%)
  between operations  14.1 us (5%)
  other arithmetic  13 us (5%)
    reduce_scatter x1, waiting for transfers between devices, body(): lax.psum_scatter(partial_value.astype(jnp.bfloat16), 'tp', scatter_dimens...  51.9 us
    all_gather x1, waiting for transfers between devices, body(): lax.all_gather(value_proj, 'ctx', axis=0, tiled=True)  46.4 us
    all_gather x1, waiting for transfers between devices, body(): lax.all_gather(key_proj, 'ctx', axis=0, tiled=True)  45.7 us
    dot_general x16, matrix products, attend_tile(): jnp.einsum('qkgn,nkd->qkgd', dropped, v_heads, preferred_element_type=jnp...  39.1 us
    dot_general x16, matrix products, attend_tile(): jnp.einsum('qkgd,nkd->qkgn', q_heads, k_heads, preferred_element_type=jnp...  21.9 us
    dynamic_slice x16, local copies, waits for them, and re-layouts, attend_tile(): k_doc = lax.dynamic_slice_in_dim(doc_ids, k_start, count)  12.2 us
    dot_general x1, matrix products, body(): jnp.dot(attention, out_weight, preferred_element_type=jnp.float32)  12.1 us
    while x48, local copies, waits for them, and re-layouts  10.1 us
  transfers between devices with their start and end apart: 3, of which 3 were waited for; matrix products, arithmetic and copies ran while one was open for 2% of the time, Pallas kernels for 0%

commit v1 on v0

--- a/solution.py
+++ b/solution.py
@@ -94,7 +94,9 @@
 
     piece = (
         lax.all_gather(key_proj, "ctx", axis=0, tiled=True),
-        lax.all_gather(value_proj, "ctx", axis=0, tiled=True),
+        jnp.concatenate(
+            lax.all_to_all(jnp.stack([value_proj] * lax.axis_size("ctx")), "ctx", 0, 0), axis=0
+        ),
     )
     final = (
         attend_range(start_state(), contexts[0], piece[0], piece[1]),

time: 274 us -> 228 us (0.83)
  waiting for transfers between devices: 145 us -> 91.9 us
  starting transfers between devices: 0.08 us -> 8.49 us
  local copies, waits for them, and re-layouts: 25.6 us -> 18 us
  matrix products: 73.1 us -> 80.1 us
    all_gather x1 -> x0, waiting for transfers between devices: 46.4 us -> none  [body(): lax.all_gather(value_proj, 'ctx', axis=0, tiled=True)]
    all_gather x1, waiting for transfers between devices: 45.7 us -> 24 us  [body(): lax.all_gather(key_proj, 'ctx', axis=0, tiled=True)]
    all_to_all x0 -> x1, waiting for transfers between devices: none -> 15.3 us  [body(): lax.all_to_all(jnp.stack([value_proj] * lax.axis_size('ctx')), 'ctx', 0, 0)]
    while x48 -> x16, local copies, waits for them, and re-layouts: 10.1 us -> 0.04 us
    all_to_all x0 -> x1, starting transfers between devices: none -> 8.45 us  [body(): lax.all_to_all(jnp.stack([value_proj] * lax.axis_size('ctx')), 'ctx', 0, 0)]
    dot_general x16, matrix products: 39.1 us -> 46.2 us  [attend_tile(): jnp.einsum('qkgn,nkd->qkgd', dropped, v_heads, preferred_element_type=jnp...]
  transfers between devices with their start and end apart: 3 -> 3, of which waited for: 3 -> 3; matrix products, arithmetic and copies ran while one was open for 2% -> 3% of each run, Pallas kernels for 0% -> 0%
where the time goes in v1:
time: 228 us; the launch traced here: 226 us
  waiting for transfers between devices  91.9 us (40%)
  matrix products  80.1 us (35%)
  local copies, waits for them, and re-layouts  18 us (8%)
  between operations  14.5 us (6%)
  other arithmetic  12.1 us (5%)
  starting transfers between devices  8.49 us (4%)
    reduce_scatter x1, waiting for transfers between devices, body(): lax.psum_scatter(partial_value.astype(jnp.bfloat16), 'tp', scatter_dimens...  51.9 us
    dot_general x16, matrix products, attend_tile(): jnp.einsum('qkgn,nkd->qkgd', dropped, v_heads, preferred_element_type=jnp...  46.2 us
    all_gather x1, waiting for transfers between devices, body(): lax.all_gather(key_proj, 'ctx', axis=0, tiled=True)  24 us
    dot_general x16, matrix products, attend_tile(): jnp.einsum('qkgd,nkd->qkgn', q_heads, k_heads, preferred_element_type=jnp...  21.8 us
    all_to_all x1, waiting for transfers between devices, body(): lax.all_to_all(jnp.stack([value_proj] * lax.axis_size('ctx')), 'ctx', 0, 0)  15.3 us
    dynamic_slice x16, local copies, waits for them, and re-layouts, attend_tile(): k_doc = lax.dynamic_slice_in_dim(doc_ids, k_start, count)  12.3 us
    dot_general x1, matrix products, body(): jnp.dot(attention, out_weight, preferred_element_type=jnp.float32)  12.1 us
    all_to_all x1, starting transfers between devices, body(): lax.all_to_all(jnp.stack([value_proj] * lax.axis_size('ctx')), 'ctx', 0, 0)  8.45 us
  transfers between devices with their start and end apart: 3, of which 3 were waited for; matrix products, arithmetic and copies ran while one was open for 3% of the time, Pallas kernels for 0%

profile of v1, /device:TPU:1, one launch (start us, length us, event | category | flops | bytes accessed | tf_op | source)
XLA Modules:
  0.0 226.2 jit_solution(11844304361821582917)
XLA Ops:
  6.5 0.7 all-gather.2.cloned.1.call-update
  7.3 0.9 copy.27
  8.2 1.1 stack.2
  9.3 8.4 %all-to-all-start = ((bf16[16,256,128]{1,2,0:T(8,128)(2,1)}), bf16[16,256,128]{1,2,0:T(8,128)(2,1)S(1)}, u32[]{:S(2)}, u32[]{:S(2)}) async-start(bf16[16,256,128]{1,2,0:T(8,128)(2,1)} %stack.2), calls=%async_computation | async-start | bytes 2097152 | tf_op jit(solution)/shard_map/all_to_all | solution.py:98
  19.6 0.9 fusion.75
  20.5 15.3 %all-to-all-done = bf16[16,256,128]{1,2,0:T(8,128)(2,1)S(1)} async-done(((bf16[16,256,128]{1,2,0:T(8,128)(2,1)}), bf16[16,256,128]{1,2,0:T(8,128)(2,1)S(1)}, u32[]{:S(2)}, u32[]{:S(2)}) %all-to-all-start) | async-done | bytes 1048608 | tf_op jit(solution)/shard_map/all_to_all | solution.py:98
  35.8 0.7 copy.28
  36.4 1.3 copy.30
  37.8 24.0 %all-gather.2.cloned.1.call-done = bf16[4096,128]{1,0:T(8,128)(2,1)} async-done(((bf16[256,128]{1,0:T(8,128)(2,1)}), bf16[4096,128]{1,0:T(8,128)(2,1)}) %all-gather.2.cloned.1.call-update) | async-done | bytes 1048592 | tf_op jit(solution)/shard_map/all_gather | solution.py:96
  61.8 50.2 %while.36 = (s32[]{:T(128)}, f32[128,1,8]{0,2,1:T(8,128)S(1)}, f32[128,1,8]{0,2,1:T(8,128)S(1)}, f32[128,1,8,128]{0,3,2,1:T(8,128)}, s32[128]{0:T(128)S(1)}, /*i...) while((s32[]{:T(128)}, f32[128,1,8]{0,2,1:T(8,128)S(1)}, ...), condition=%wide.region_3.4_spmd.clone, body=%wide.region_0.3_spmd.clone.sunk | while | flops 281624192 | bytes 8214787 | solution.py:61
  61.8 0.8 dynamic_slice.86
  62.8 1.4 fusion.93
  64.3 3.2 %fusion.97 = f32[128,1,8,128]{0,3,2,1:T(8,128)} fusion(f32[512,128,8]{1,0,2:T(8,128)S(1)} %get-tuple-element.747, s32[512]{0:T(512)S(1)} %iota_add_fusion.11, s32[128,8]{0,1:T(8,128)S(1)} %fusion.96, f32[128,8]{0,1:T(8,128)S(1)} %bitcast.162, pred[128,512]{0,1:T(8,128)(4,1)S(1)} %compare_and_fusion.4, f32[128,1,8,128]{0,3,2,1:T(8,128)} %get-tuple-element.832, ...), kind=kOutput, calls=%fused_computation.19.clone.1 | convolution fusion | flops 143523840 | bytes 3356677 | tf_op jit(solution)/shard_map/while/body/eval_jaxpr/qkgn,nkd->qkgd/dot_general | solution.py:45
  67.9 0.8 dynamic_slice.86
  68.9 1.4 fusion.93
  70.3 3.4 %fusion.97 = f32[128,1,8,128]{0,3,2,1:T(8,128)} fusion(f32[512,128,8]{1,0,2:T(8,128)S(1)} %get-tuple-element.747, s32[512]{0:T(512)S(1)} %iota_add_fusion.11, s32[128,8]{0,1:T(8,128)S(1)} %fusion.96, f32[128,8]{0,1:T(8,128)S(1)} %bitcast.162, pred[128,512]{0,1:T(8,128)(4,1)S(1)} %compare_and_fusion.4, f32[128,1,8,128]{0,3,2,1:T(8,128)} %get-tuple-element.832, ...), kind=kOutput, calls=%fused_computation.19.clone.1 | convolution fusion | flops 143523840 | bytes 3356677 | tf_op jit(solution)/shard_map/while/body/eval_jaxpr/qkgn,nkd->qkgd/dot_general | solution.py:45
  74.2 0.8 dynamic_slice.86
  75.2 1.4 fusion.93
  76.6 3.4 %fusion.97 = f32[128,1,8,128]{0,3,2,1:T(8,128)} fusion(f32[512,128,8]{1,0,2:T(8,128)S(1)} %get-tuple-element.747, s32[512]{0:T(512)S(1)} %iota_add_fusion.11, s32[128,8]{0,1:T(8,128)S(1)} %fusion.96, f32[128,8]{0,1:T(8,128)S(1)} %bitcast.162, pred[128,512]{0,1:T(8,128)(4,1)S(1)} %compare_and_fusion.4, f32[128,1,8,128]{0,3,2,1:T(8,128)} %get-tuple-element.832, ...), kind=kOutput, calls=%fused_computation.19.clone.1 | convolution fusion | flops 143523840 | bytes 3356677 | tf_op jit(solution)/shard_map/while/body/eval_jaxpr/qkgn,nkd->qkgd/dot_general | solution.py:45
  80.5 0.8 dynamic_slice.86
  81.5 1.4 fusion.93
  83.0 3.4 %fusion.97 = f32[128,1,8,128]{0,3,2,1:T(8,128)} fusion(f32[512,128,8]{1,0,2:T(8,128)S(1)} %get-tuple-element.747, s32[512]{0:T(512)S(1)} %iota_add_fusion.11, s32[128,8]{0,1:T(8,128)S(1)} %fusion.96, f32[128,8]{0,1:T(8,128)S(1)} %bitcast.162, pred[128,512]{0,1:T(8,128)(4,1)S(1)} %compare_and_fusion.4, f32[128,1,8,128]{0,3,2,1:T(8,128)} %get-tuple-element.832, ...), kind=kOutput, calls=%fused_computation.19.clone.1 | convolution fusion | flops 143523840 | bytes 3356677 | tf_op jit(solution)/shard_map/while/body/eval_jaxpr/qkgn,nkd->qkgd/dot_general | solution.py:45
  86.8 0.8 dynamic_slice.86
  87.8 1.4 fusion.93
  89.3 3.4 %fusion.97 = f32[128,1,8,128]{0,3,2,1:T(8,128)} fusion(f32[512,128,8]{1,0,2:T(8,128)S(1)} %get-tuple-element.747, s32[512]{0:T(512)S(1)} %iota_add_fusion.11, s32[128,8]{0,1:T(8,128)S(1)} %fusion.96, f32[128,8]{0,1:T(8,128)S(1)} %bitcast.162, pred[128,512]{0,1:T(8,128)(4,1)S(1)} %compare_and_fusion.4, f32[128,1,8,128]{0,3,2,1:T(8,128)} %get-tuple-element.832, ...), kind=kOutput, calls=%fused_computation.19.clone.1 | convolution fusion | flops 143523840 | bytes 3356677 | tf_op jit(solution)/shard_map/while/body/eval_jaxpr/qkgn,nkd->qkgd/dot_general | solution.py:45
  93.1 0.8 dynamic_slice.86
  94.1 1.4 fusion.93
  95.6 3.4 %fusion.97 = f32[128,1,8,128]{0,3,2,1:T(8,128)} fusion(f32[512,128,8]{1,0,2:T(8,128)S(1)} %get-tuple-element.747, s32[512]{0:T(512)S(1)} %iota_add_fusion.11, s32[128,8]{0,1:T(8,128)S(1)} %fusion.96, f32[128,8]{0,1:T(8,128)S(1)} %bitcast.162, pred[128,512]{0,1:T(8,128)(4,1)S(1)} %compare_and_fusion.4, f32[128,1,8,128]{0,3,2,1:T(8,128)} %get-tuple-element.832, ...), kind=kOutput, calls=%fused_computation.19.clone.1 | convolution fusion | flops 143523840 | bytes 3356677 | tf_op jit(solution)/shard_map/while/body/eval_jaxpr/qkgn,nkd->qkgd/dot_general | solution.py:45
  99.4 0.8 dynamic_slice.86
  100.4 1.4 fusion.93
  101.9 3.4 %fusion.97 = f32[128,1,8,128]{0,3,2,1:T(8,128)} fusion(f32[512,128,8]{1,0,2:T(8,128)S(1)} %get-tuple-element.747, s32[512]{0:T(512)S(1)} %iota_add_fusion.11, s32[128,8]{0,1:T(8,128)S(1)} %fusion.96, f32[128,8]{0,1:T(8,128)S(1)} %bitcast.162, pred[128,512]{0,1:T(8,128)(4,1)S(1)} %compare_and_fusion.4, f32[128,1,8,128]{0,3,2,1:T(8,128)} %get-tuple-element.832, ...), kind=kOutput, calls=%fused_computation.19.clone.1 | convolution fusion | flops 143523840 | bytes 3356677 | tf_op jit(solution)/shard_map/while/body/eval_jaxpr/qkgn,nkd->qkgd/dot_general | solution.py:45
  105.7 0.8 dynamic_slice.86
  106.7 1.4 fusion.93
  108.2 3.4 %fusion.97 = f32[128,1,8,128]{0,3,2,1:T(8,128)} fusion(f32[512,128,8]{1,0,2:T(8,128)S(1)} %get-tuple-element.747, s32[512]{0:T(512)S(1)} %iota_add_fusion.11, s32[128,8]{0,1:T(8,128)S(1)} %fusion.96, f32[128,8]{0,1:T(8,128)S(1)} %bitcast.162, pred[128,512]{0,1:T(8,128)(4,1)S(1)} %compare_and_fusion.4, f32[128,1,8,128]{0,3,2,1:T(8,128)} %get-tuple-element.832, ...), kind=kOutput, calls=%fused_computation.19.clone.1 | convolution fusion | flops 143523840 | bytes 3356677 | tf_op jit(solution)/shard_map/while/body/eval_jaxpr/qkgn,nkd->qkgd/dot_general | solution.py:45
  112.0 43.2 %while.37 = (s32[]{:T(128)}, f32[128,1,8]{0,2,1:T(8,128)S(1)}, f32[128,1,8]{0,2,1:T(8,128)S(1)}, f32[128,1,8,128]{0,3,2,1:T(8,128)S(1)}, s32[128]{0:T(128)S(1)},...) while((s32[]{:T(128)}, f32[128,1,8]{0,2,1:T(8,128)S(1)}, ...), condition=%wide.region_7.8_spmd.clone, body=%wide.region_4.7_spmd.clone.sunk | while | flops 281624192 | bytes 8214787 | solution.py:61
  112.0 0.8 dynamic_slice.89
  113.1 1.4 fusion.100
  114.5 2.4 %fusion.104 = f32[128,1,8,128]{0,3,2,1:T(8,128)S(1)} fusion(f32[512,128,8]{1,0,2:T(8,128)S(1)} %get-tuple-element.763, s32[512]{0:T(512)S(1)} %iota_add_fusion.13, s32[128,8]{0,1:T(8,128)S(1)} %fusion.103, f32[128,8]{0,1:T(8,128)S(1)} %bitcast.164, pred[128,512]{0,1:T(8,128)(4,1)S(1)} %compare_and_fusion.5, ...), kind=kOutput, calls=%fused_computation.67.clone.1 | convolution fusion | flops 143523840 | bytes 3356677 | tf_op jit(solution)/shard_map/while/body/eval_jaxpr/qkgn,nkd->qkgd/dot_general | solution.py:45
  117.5 0.8 dynamic_slice.89
  118.5 1.4 fusion.100
  119.9 2.4 %fusion.104 = f32[128,1,8,128]{0,3,2,1:T(8,128)S(1)} fusion(f32[512,128,8]{1,0,2:T(8,128)S(1)} %get-tuple-element.763, s32[512]{0:T(512)S(1)} %iota_add_fusion.13, s32[128,8]{0,1:T(8,128)S(1)} %fusion.103, f32[128,8]{0,1:T(8,128)S(1)} %bitcast.164, pred[128,512]{0,1:T(8,128)(4,1)S(1)} %compare_and_fusion.5, ...), kind=kOutput, calls=%fused_computation.67.clone.1 | convolution fusion | flops 143523840 | bytes 3356677 | tf_op jit(solution)/shard_map/while/body/eval_jaxpr/qkgn,nkd->qkgd/dot_general | solution.py:45
  122.9 0.8 dynamic_slice.89
  123.9 1.4 fusion.100
  125.3 2.4 %fusion.104 = f32[128,1,8,128]{0,3,2,1:T(8,128)S(1)} fusion(f32[512,128,8]{1,0,2:T(8,128)S(1)} %get-tuple-element.763, s32[512]{0:T(512)S(1)} %iota_add_fusion.13, s32[128,8]{0,1:T(8,128)S(1)} %fusion.103, f32[128,8]{0,1:T(8,128)S(1)} %bitcast.164, pred[128,512]{0,1:T(8,128)(4,1)S(1)} %compare_and_fusion.5, ...), kind=kOutput, calls=%fused_computation.67.clone.1 | convolution fusion | flops 143523840 | bytes 3356677 | tf_op jit(solution)/shard_map/while/body/eval_jaxpr/qkgn,nkd->qkgd/dot_general | solution.py:45
  128.3 0.8 dynamic_slice.89
  129.2 1.4 fusion.100
  130.7 2.4 %fusion.104 = f32[128,1,8,128]{0,3,2,1:T(8,128)S(1)} fusion(f32[512,128,8]{1,0,2:T(8,128)S(1)} %get-tuple-element.763, s32[512]{0:T(512)S(1)} %iota_add_fusion.13, s32[128,8]{0,1:T(8,128)S(1)} %fusion.103, f32[128,8]{0,1:T(8,128)S(1)} %bitcast.164, pred[128,512]{0,1:T(8,128)(4,1)S(1)} %compare_and_fusion.5, ...), kind=kOutput, calls=%fused_computation.67.clone.1 | convolution fusion | flops 143523840 | bytes 3356677 | tf_op jit(solution)/shard_map/while/body/eval_jaxpr/qkgn,nkd->qkgd/dot_general | solution.py:45
  133.7 0.8 dynamic_slice.89
  134.6 1.4 fusion.100
  136.1 2.4 %fusion.104 = f32[128,1,8,128]{0,3,2,1:T(8,128)S(1)} fusion(f32[512,128,8]{1,0,2:T(8,128)S(1)} %get-tuple-element.763, s32[512]{0:T(512)S(1)} %iota_add_fusion.13, s32[128,8]{0,1:T(8,128)S(1)} %fusion.103, f32[128,8]{0,1:T(8,128)S(1)} %bitcast.164, pred[128,512]{0,1:T(8,128)(4,1)S(1)} %compare_and_fusion.5, ...), kind=kOutput, calls=%fused_computation.67.clone.1 | convolution fusion | flops 143523840 | bytes 3356677 | tf_op jit(solution)/shard_map/while/body/eval_jaxpr/qkgn,nkd->qkgd/dot_general | solution.py:45
  139.1 0.8 dynamic_slice.89
  140.0 1.4 fusion.100
  141.5 2.4 %fusion.104 = f32[128,1,8,128]{0,3,2,1:T(8,128)S(1)} fusion(f32[512,128,8]{1,0,2:T(8,128)S(1)} %get-tuple-element.763, s32[512]{0:T(512)S(1)} %iota_add_fusion.13, s32[128,8]{0,1:T(8,128)S(1)} %fusion.103, f32[128,8]{0,1:T(8,128)S(1)} %bitcast.164, pred[128,512]{0,1:T(8,128)(4,1)S(1)} %compare_and_fusion.5, ...), kind=kOutput, calls=%fused_computation.67.clone.1 | convolution fusion | flops 143523840 | bytes 3356677 | tf_op jit(solution)/shard_map/while/body/eval_jaxpr/qkgn,nkd->qkgd/dot_general | solution.py:45
  144.0 0.4 fusion.102
  144.4 0.8 dynamic_slice.89
  145.4 1.4 fusion.100
  146.9 2.4 %fusion.104 = f32[128,1,8,128]{0,3,2,1:T(8,128)S(1)} fusion(f32[512,128,8]{1,0,2:T(8,128)S(1)} %get-tuple-element.763, s32[512]{0:T(512)S(1)} %iota_add_fusion.13, s32[128,8]{0,1:T(8,128)S(1)} %fusion.103, f32[128,8]{0,1:T(8,128)S(1)} %bitcast.164, pred[128,512]{0,1:T(8,128)(4,1)S(1)} %compare_and_fusion.5, ...), kind=kOutput, calls=%fused_computation.67.clone.1 | convolution fusion | flops 143523840 | bytes 3356677 | tf_op jit(solution)/shard_map/while/body/eval_jaxpr/qkgn,nkd->qkgd/dot_general | solution.py:45
  149.3 0.4 fusion.102
  149.8 0.8 dynamic_slice.89
  150.8 1.4 fusion.100
  152.3 2.4 %fusion.104 = f32[128,1,8,128]{0,3,2,1:T(8,128)S(1)} fusion(f32[512,128,8]{1,0,2:T(8,128)S(1)} %get-tuple-element.763, s32[512]{0:T(512)S(1)} %iota_add_fusion.13, s32[128,8]{0,1:T(8,128)S(1)} %fusion.103, f32[128,8]{0,1:T(8,128)S(1)} %bitcast.164, pred[128,512]{0,1:T(8,128)(4,1)S(1)} %compare_and_fusion.5, ...), kind=kOutput, calls=%fused_computation.67.clone.1 | convolution fusion | flops 143523840 | bytes 3356677 | tf_op jit(solution)/shard_map/while/body/eval_jaxpr/qkgn,nkd->qkgd/dot_general | solution.py:45
  154.7 0.4 fusion.102
  155.3 12.1 %convolution_convert_fusion = bf16[256,8192]{1,0:T(8,128)(2,1)} fusion(bf16[1024,8192]{1,0:T(8,128)(2,1)} %param.13, bf16[128,1024]{0,1:T(8,128)(2,1)S(1)} %bitcast.167, bf16[128,1024]{0,1:T(8,128)(2,1)S(1)} %bitcast.166), kind=kOutput, calls=%fused_computation.100 | convolution fusion | flops 4298113024 | bytes 21495808 | tf_op jit(solution)/shard_map/dot_general | solution.py:115
  167.5 51.9 %reduce-scatter.2.cloned.1.call-done = bf16[256,1024]{1,0:T(8,128)(2,1)} async-done(((bf16[256,8192]{1,0:T(8,128)(2,1)}), bf16[256,1024]{1,0:T(8,128)(2,1)}) %reduce-scatter.2.cloned.1.call-update) | async-done | bytes 524304 | tf_op jit(solution)/shard_map/reduce_scatter | solution.py:116
  (150 shorter events, 11.6 us)
Async XLA Ops:
  6.5 12.2 %copy-start.1 = (bf16[256,1024]{1,0:T(8,128)(2,1)S(1)}, bf16[256,1024]{1,0:T(8,128)(2,1)}, u32[]{:S(2)}) copy-start(bf16[256,1024]{1,0:T(8,128)(2,1)} %param.10) | copy-start | bytes 1572868
  6.5 55.3 %all-gather.2.cloned.1.call-start = ((), (), s32[]{:S(2)}) async-start(), calls=%async_computation.2 | async-start | bytes 1114112 | tf_op jit(solution)/shard_map/all_gather | solution.py:96
  9.3 26.4 %all-to-all-start = ((bf16[16,256,128]{1,2,0:T(8,128)(2,1)}), bf16[16,256,128]{1,2,0:T(8,128)(2,1)S(1)}, u32[]{:S(2)}, u32[]{:S(2)}) async-start(bf16[16,256,128]{1,2,0:T(8,128)(2,1)} %stack.2), calls=%async_computation | async-start | bytes 2097152 | tf_op jit(solution)/shard_map/all_to_all | solution.py:98
  17.8 201.6 %reduce-scatter.2.cloned.1.call-start = ((), (), s32[]{:S(2)}) async-start(), calls=%async_computation.3 | async-start | bytes 4718592 | tf_op jit(solution)/shard_map/reduce_scatter | solution.py:116
  112.0 43.2 %copy-start = (f32[128,1,8,128]{0,3,2,1:T(8,128)S(1)}, f32[128,1,8,128]{0,3,2,1:T(8,128)}, u32[]{:S(2)}) copy-start(f32[128,1,8,128]{0,3,2,1:T(8,128)} %get-tuple-element.375) | copy-start | bytes 1572868
Sparse Core Ops, SparseCore 0:
  9.8 52.0 all-gather.1
  167.6 51.7 reduce-scatter.1
